TPU v7x, 512 devices: a whole 4x8x8 slice. The times are simulated.
512 devices in a mesh: grp: 64 (over y, z), tp: 8 (over x, core).
Axes of the slice: x: 4, y: 8, z: 8, core: 2. Of those that a mesh axis runs over, the one named last changes fastest.
Arguments:
- queries: bfloat16 [512, 2048], P('grp', 'tp'), may hold values from -8 to 8
- new_kv: bfloat16 [512, 2, 512], P('grp', None, 'tp'), may hold values from -6 to 6
- home_cache: bfloat16 [512, 2, 8, 512, 128], P('grp', None, 'tp'), may hold values from -28 to 28
- help_cache: bfloat16 [256, 2, 8, 512, 128], P('grp', None, 'tp'), may hold values from -6 to 6
- lengths: int32 [512], P('grp'), may hold values from 2 to 2048, as said below
- split_at: int32 [512], P('grp'), may hold values from 1 to 1024, as said below
- helper_req: int32 [256], P('grp'), may hold values from 0 to 511, as said below
- out_weight: bfloat16 [2048, 2048], P('tp'), may hold values from -0.125 to 0.125
Outputs:
- attn_out: bfloat16 [512, 2048], P('grp', 'tp')
Inputs may be any that keep to these rules, and one draw needn't show every extreme that they name: `lengths`: in each aligned block of 8 requests exactly 4 have more than 1024 cached positions. `split_at`: equal to the length for requests of 1024 positions or fewer; otherwise between length - 1024 and min(1024, length - 1). `helper_req`: groups come in pairs; the 4 helper slots of a group serve, in increasing order, the requests of its partner group that have more than 1024 positions, so each such request has exactly one helper slot and all values are distinct.
All inputs are finite; a program needn't handle non-finite values.
Results may differ from a plain program's by a relative error of at most 0.007.
Values may be sent and summed in bfloat16 or wider, within the bound.
A program may use at most 192 MiB of HBM per device.

v0:
```python
import jax
import jax.numpy as jnp
from jax import lax
from jax.sharding import PartitionSpec as P


def attend(queries, cache, count, fresh):
    row_count = queries.shape[0]
    kv_heads = cache.shape[2]
    head_width = cache.shape[4] // 2
    context = cache.shape[3] * 2
    group_size = queries.shape[1] // (kv_heads * head_width)
    score_scale = head_width ** (-0.5)
    head_rows = queries.reshape(row_count, kv_heads, group_size, head_width)
    key_rows = cache[:, 0].reshape(row_count, kv_heads, context, head_width)
    value_rows = cache[:, 1].reshape(row_count, kv_heads, context, head_width)
    scores = (
        jnp.einsum("nkgd,nkpd->nkgp", head_rows, key_rows, preferred_element_type=jnp.float32)
        * score_scale
    )
    inside = (jnp.arange(context)[None, :] < count[:, None])[:, None, None, :]
    top_score = jnp.max(jnp.where(inside, scores, -1e30), axis=-1)
    if fresh is not None:
        fresh_key = fresh[:, 0].reshape(row_count, kv_heads, head_width)
        fresh_score = (
            jnp.einsum("nkgd,nkd->nkg", head_rows, fresh_key, preferred_element_type=jnp.float32)
            * score_scale
        )
        top_score = jnp.maximum(top_score, fresh_score)
    weights = jnp.where(inside, jnp.exp(scores - top_score[..., None]), 0.0).astype(jnp.bfloat16)
    weight_sum = jnp.sum(weights.astype(jnp.float32), axis=-1)
    mixed_sum = jnp.einsum(
        "nkgp,nkpd->nkgd", weights, value_rows, preferred_element_type=jnp.float32
    )
    if fresh is not None:
        fresh_weight = lax.optimization_barrier(
            jnp.exp(fresh_score - top_score).astype(jnp.bfloat16)
        ).astype(jnp.float32)
        weight_sum = weight_sum + fresh_weight
        fresh_value = fresh[:, 1].reshape(row_count, kv_heads, 1, head_width).astype(jnp.float32)
        mixed_sum = mixed_sum + fresh_weight[..., None] * fresh_value
    return (
        top_score.reshape(row_count, -1),
        weight_sum.reshape(row_count, -1),
        mixed_sum.reshape(row_count, -1, head_width),
    )


def per_device(queries, new_kv, home_cache, help_cache, lengths, split_at, helper_req, out_weight):
    row_count = queries.shape[0]
    total_rows = row_count * lax.axis_size("grp")
    row_ids = jnp.arange(total_rows)
    help_sel = helper_req[:, None] == row_ids[None, :]
    everyone, all_lengths, all_splits = (
        lax.all_gather(queries, "grp", axis=0, tiled=True),
        lax.all_gather(lengths, "grp", axis=0, tiled=True),
        lax.all_gather(split_at, "grp", axis=0, tiled=True),
    )
    help_queries = jnp.dot(
        help_sel.astype(jnp.bfloat16), everyone, preferred_element_type=jnp.float32
    ).astype(jnp.bfloat16)
    help_count = jnp.sum(jnp.where(help_sel, (all_lengths - all_splits)[None, :], 0), axis=1)
    home_m, home_l, home_u = attend(queries, home_cache, split_at, new_kv)
    help_m, help_l, help_u = attend(help_queries, help_cache, help_count, None)
    row_start = lax.axis_index("grp") * row_count
    all_m, all_l, all_u, all_req = (
        lax.all_gather(help_m, "grp", axis=0, tiled=True),
        lax.all_gather(help_l, "grp", axis=0, tiled=True),
        lax.all_gather(help_u, "grp", axis=0, tiled=True),
        lax.all_gather(helper_req, "grp", axis=0, tiled=True),
    )
    own_ids = row_start + jnp.arange(row_count)
    own_sel = own_ids[:, None] == all_req[None, :]
    far_m = jnp.max(jnp.where(own_sel[:, :, None], all_m[None], -1e30), axis=1)
    far_l = jnp.sum(jnp.where(own_sel[:, :, None], all_l[None], 0.0), axis=1)
    far_u = jnp.sum(jnp.where(own_sel[:, :, None, None], all_u[None], 0.0), axis=1)
    top_score = jnp.maximum(home_m, far_m)
    home_e = jnp.exp(home_m - top_score)
    far_e = jnp.exp(far_m - top_score)
    numerator = home_u * home_e[..., None] + far_u * far_e[..., None]
    denominator = home_l * home_e + far_l * far_e
    heads_out = numerator / denominator[..., None]
    mix = heads_out.reshape(row_count, -1).astype(jnp.bfloat16)
    partial_out = jnp.dot(mix, out_weight, preferred_element_type=jnp.float32)
    return lax.psum_scatter(partial_out, "tp", scatter_dimension=1, tiled=True).astype(jnp.bfloat16)


def solution(mesh):
    return jax.shard_map(
        per_device,
        mesh=mesh,
        in_specs=(
            P("grp", "tp"),
            P("grp", None, "tp"),
            P("grp", None, "tp", None, None),
            P("grp", None, "tp", None, None),
            P("grp"),
            P("grp"),
            P("grp"),
            P("tp", None),
        ),
        out_specs=P("grp", "tp"),
        check_vma=False,
    )
```

profile of v0, /device:TPU:8, one launch (start us, length us, event | category | flops | bytes accessed | tf_op | source)
XLA Modules:
  0.0 292.7 jit_solution(9021844830264315112)
XLA Ops:
  6.5 0.0 reduce-scatter.2.cloned.1.call-start
  6.5 0.9 reshape.232
  7.4 55.8 %all_gather.24 = bf16[512,256]{1,0:T(8,128)(2,1)S(1)} all-gather(bf16[8,256]{1,0:T(8,128)(2,1)} %param.8), channel_id=1, replica_groups=mesh['grp'=64,'tp'=8] {'grp'}, dimensions={0}, use_global_device_ids=true | all-gather | bytes 266240 | tf_op jit(solution)/shard_map/all_gather | solution.py:55
  63.2 1.3 dynamic-slice
  65.7 0.7 iota_compare_fusion
  66.5 0.8 dynamic-update-slice.2
  67.3 0.8 dynamic-update-slice.1
  68.1 0.8 dynamic-update-slice
  69.0 22.3 %all-reduce.3 = (s32[512]{0:T(512)S(1)}, s32[512]{0:T(512)S(1)}, s32[256]{0:T(256)S(1)}) all-reduce(s32[512]{0:T(512)S(1)} %dynamic-update-slice.1, s32[512]{0:T(512)S(1)} %dynamic-update-slice.2, s32[256]{0:T(256)S(1)} %dynamic-update-slice), channel_id=1, replica_groups=mesh['grp'=64,'tp'=8] {'grp'}, use_global_device_ids=true, to_apply=%add.1 | all-reduce | flops 1280 | bytes 10240
  91.3 0.8 select_reduce_fusion.5
  92.1 0.1 iota_compare_fusion.1
  92.2 0.8 slice_convert_fusion
  93.0 0.8 convolution_convert_fusion
  93.8 0.1 reshape.236
  93.9 1.3 fusion.14
  95.2 0.4 reshape.237
  95.6 0.5 select_reduce_fusion.2
  96.1 0.2 convert_reduce_fusion.1
  96.2 46.9 %all-gather.1 = f32[64,4,4]{2,1,0:T(4,128)S(1)} all-gather(f32[1,4,4]{2,1,0:T(4,128)S(1)} %bitcast.43), channel_id=1, replica_groups=mesh['grp'=64,'tp'=8] {'grp'}, dimensions={0}, use_global_device_ids=true | all-gather | bytes 4160 | tf_op jit(solution)/shard_map/all_gather | solution.py:68
  143.2 0.1 copy.46
  143.2 47.7 %all-gather = f32[64,4,4]{2,1,0:T(4,128)S(1)} all-gather(f32[1,4,4]{2,1,0:T(4,128)S(1)} %bitcast.40), channel_id=1, replica_groups=mesh['grp'=64,'tp'=8] {'grp'}, dimensions={0}, use_global_device_ids=true | all-gather | bytes 4160 | tf_op jit(solution)/shard_map/all_gather | solution.py:67
  190.9 0.1 copy.39
  191.0 0.1 broadcast_compare_fusion
  191.1 0.1 select_reduce_fusion.4
  191.2 0.1 copy.40
  191.3 0.1 copy.47
  191.4 0.4 reshape.238
  191.8 0.3 fusion.10
  192.1 47.3 %all_gather.26 = f32[256,4,64]{2,1,0:T(4,128)S(1)} all-gather(f32[4,4,64]{2,1,0:T(4,128)S(1)} %fusion.10), channel_id=1, replica_groups=mesh['grp'=64,'tp'=8] {'grp'}, dimensions={0}, use_global_device_ids=true | all-gather | bytes 266240 | tf_op jit(solution)/shard_map/all_gather | solution.py:69
  239.4 0.2 copy.42
  239.6 0.4 select_reduce_fusion
  240.0 3.1 %fusion.13 = (bf16[8,1,1,512,128]{4,3,2,1,0:T(8,128)(2,1)}, bf16[8,1,1,512,128]{4,3,2,1,0:T(8,128)(2,1)}) fusion(bf16[8,2,1,512,128]{4,3,2,1,0:T(8,128)(2,1)} %param.10), kind=kLoop, calls=%fused_computation.39 | loop fusion | bytes 4194304 | tf_op jit(solution)/shard_map/slice | solution.py:15
  243.1 2.7 reshape.233
  245.8 0.1 fusion.7
  245.9 0.7 select_reduce_fusion.1
  246.7 0.1 copy.36
  246.8 0.1 copy.37
  246.9 0.2 convert_reduce_fusion
  247.1 0.1 copy.44
  247.2 0.1 copy.45
  247.3 2.7 reshape.235
  250.1 0.4 fusion.3
  250.5 0.1 convert_element_type.60
  250.6 0.0 copy-done
  250.6 0.9 fusion.15
  251.5 0.0 reduce-scatter.2.cloned.1.call-update
  251.5 33.1 %reduce-scatter.2.cloned.1.call-done = f32[8,256]{1,0:T(8,128)} async-done(((f32[8,2048]{1,0:T(8,128)}), f32[8,256]{1,0:T(8,128)}) %reduce-scatter.2.cloned.1.call-update) | async-done | bytes 8208 | tf_op jit(solution)/shard_map/reduce_scatter | solution.py:85
  284.6 1.3 convert_element_type.61
  (11 shorter events, 0.1 us)
Async XLA Ops:
  6.5 244.1 %copy-start = (bf16[256,2048]{1,0:T(8,128)(2,1)S(1)}, bf16[256,2048]{1,0:T(8,128)(2,1)}, u32[]{:S(2)}) copy-start(bf16[256,2048]{1,0:T(8,128)(2,1)} %param.15) | copy-start | bytes 3145732
  6.5 278.0 %reduce-scatter.2.cloned.1.call-start = ((), (), s32[]{:S(2)}) async-start(), calls=%async_computation.1 | async-start | bytes 73728 | tf_op jit(solution)/shard_map/reduce_scatter | solution.py:85
Sparse Core Ops, SparseCore 0:
  251.6 32.9 reduce-scatter.1
where the time goes:
time: 293 us
  blocking collectives  220 us (75%)
  waiting for transfers between devices  33.1 us (11%)
  local copies, waits for them, and re-layouts  16.4 us (6%)
  between operations  14.8 us (5%)
  other arithmetic  4.71 us (2%)
  matrix products  3.79 us (1%)
    all_gather x1, blocking collectives, per_device(): lax.all_gather(queries, 'grp', axis=0, tiled=True)  55.8 us
    all_gather x1, blocking collectives, per_device(): lax.all_gather(help_m, 'grp', axis=0, tiled=True)  47.7 us
    all_gather x1, blocking collectives, per_device(): lax.all_gather(help_u, 'grp', axis=0, tiled=True)  47.3 us
    all_gather x1, blocking collectives, per_device(): lax.all_gather(help_l, 'grp', axis=0, tiled=True)  46.9 us
    reduce_scatter x1, waiting for transfers between devices, per_device(): lax.psum_scatter(partial_out, 'tp', scatter_dimension=1, tiled=True)  33.1 us
    unnamed x1, blocking collectives  22.3 us
    another operation x6, local copies, waits for them, and re-layouts  7.24 us
  transfers between devices with their start and end apart: 1, of which 1 were waited for; matrix products, arithmetic and copies ran while one was open for 0% of the time, Pallas kernels for 0%

commit v1 on v0

--- a/solution.py
+++ b/solution.py
@@ -66,7 +66,9 @@
     all_m, all_l, all_u, all_req = (
         lax.all_gather(help_m, "grp", axis=0, tiled=True),
         lax.all_gather(help_l, "grp", axis=0, tiled=True),
-        lax.all_gather(help_u, "grp", axis=0, tiled=True),
+        jnp.concatenate(
+            lax.all_to_all(jnp.stack([help_u] * lax.axis_size("grp")), "grp", 0, 0), axis=0
+        ),
         lax.all_gather(helper_req, "grp", axis=0, tiled=True),
     )
     own_ids = row_start + jnp.arange(row_count)

time: 293 us -> 271 us (0.925)
  blocking collectives: 220 us -> 175 us
  local copies, waits for them, and re-layouts: 16.4 us -> 26.8 us
  starting transfers between devices: 0.01 us -> 8.33 us
    all_gather x1 -> x0, blocking collectives: 47.3 us -> none  [per_device(): lax.all_gather(help_u, 'grp', axis=0, tiled=True)]
    unnamed x1, blocking collectives: 22.3 us -> 31.1 us
    all_gather x1, blocking collectives: 55.8 us -> 47 us  [per_device(): lax.all_gather(queries, 'grp', axis=0, tiled=True)]
    all_to_all x0 -> x1, starting transfers between devices: none -> 8.29 us  [per_device(): lax.all_to_all(jnp.stack([help_u] * lax.axis_size('grp')), 'grp', 0, 0)]
    unnamed x12 -> x27, local copies, waits for them, and re-layouts: 3.95 us -> 7.2 us
  transfers between devices with their start and end apart: 1 -> 2, of which waited for: 1 -> 1; matrix products, arithmetic and copies ran while one was open for 0% -> 6% of each run, Pallas kernels for 0% -> 0%
where the time goes in v1:
time: 271 us
  blocking collectives  175 us (65%)
  waiting for transfers between devices  34.4 us (13%)
  local copies, waits for them, and re-layouts  26.8 us (10%)
  between operations  14.9 us (5%)
  starting transfers between devices  8.33 us (3%)
  other arithmetic  7.35 us (3%)
  matrix products  4.5 us (2%)
    all_gather x1, blocking collectives, per_device(): lax.all_gather(help_l, 'grp', axis=0, tiled=True)  49 us
    all_gather x1, blocking collectives, per_device(): lax.all_gather(help_m, 'grp', axis=0, tiled=True)  47.4 us
    all_gather x1, blocking collectives, per_device(): lax.all_gather(queries, 'grp', axis=0, tiled=True)  47 us
    reduce_scatter x1, waiting for transfers between devices, per_device(): lax.psum_scatter(partial_out, 'tp', scatter_dimension=1, tiled=True)  34.4 us
    unnamed x1, blocking collectives  31.1 us
    all_to_all x1, starting transfers between devices, per_device(): lax.all_to_all(jnp.stack([help_u] * lax.axis_size('grp')), 'grp', 0, 0)  8.29 us
    another operation x6, local copies, waits for them, and re-layouts  7.7 us
    unnamed x27, local copies, waits for them, and re-layouts  7.2 us
  transfers between devices with their start and end apart: 2, of which 1 were waited for; matrix products, arithmetic and copies ran while one was open for 6% of the time, Pallas kernels for 0%

profile of v1, /device:TPU:8, one launch (start us, length us, event | category | flops | bytes accessed | tf_op | source)
XLA Modules:
  0.0 270.7 jit_solution(14226487510436149355)
XLA Ops:
  6.5 1.4 dynamic-slice
  9.2 0.9 dynamic-update-slice.1
  10.1 0.8 dynamic-update-slice.2
  10.9 0.8 dynamic-update-slice
  11.7 31.1 %all-reduce.3 = (s32[512]{0:T(512)S(1)}, s32[512]{0:T(512)S(1)}, s32[256]{0:T(256)S(1)}) all-reduce(s32[512]{0:T(512)S(1)} %dynamic-update-slice.1, s32[512]{0:T(512)S(1)} %dynamic-update-slice.2, s32[256]{0:T(256)S(1)} %dynamic-update-slice), channel_id=1, replica_groups=mesh['grp'=64,'tp'=8] {'grp'}, use_global_device_ids=true, to_apply=%add.1 | all-reduce | flops 1280 | bytes 10240
  42.8 0.8 select_reduce_fusion.5
  43.7 47.0 %all_gather.21 = bf16[512,256]{1,0:T(8,128)(2,1)S(1)} all-gather(bf16[8,256]{1,0:T(8,128)(2,1)} %param.8), channel_id=1, replica_groups=mesh['grp'=64,'tp'=8] {'grp'}, dimensions={0}, use_global_device_ids=true | all-gather | bytes 266240 | tf_op jit(solution)/shard_map/all_gather | solution.py:55
  90.7 0.8 convolution_convert_fusion
  91.5 0.1 reshape.237
  91.6 2.1 fusion.14
  93.7 0.4 reshape.238
  94.1 1.6 reshape.239
  95.8 0.5 select_reduce_fusion.2
  96.3 0.3 fusion.10
  96.6 0.1 broadcast_bitcast_fusion
  96.7 1.2 reshape.263
  97.9 8.3 %all-to-all-start = ((f32[64,1,1024]{2,1,0:T(1,128)}), f32[64,1,1024]{2,1,0:T(1,128)S(1)}, u32[]{:S(2)}, u32[]{:S(2)}) async-start(f32[64,1,1024]{2,1,0:T(1,128)} %reshape.263), calls=%async_computation | async-start | bytes 524288 | tf_op jit(solution)/shard_map/all_to_all | solution.py:70
  106.3 0.1 reshape.233
  106.4 0.2 convert_reduce_fusion.1
  106.6 0.6 slice_convert_fusion
  107.2 49.0 %all-gather.1 = f32[64,4,4]{2,1,0:T(4,128)S(1)} all-gather(f32[1,4,4]{2,1,0:T(4,128)S(1)} %bitcast.49), channel_id=1, replica_groups=mesh['grp'=64,'tp'=8] {'grp'}, dimensions={0}, use_global_device_ids=true | all-gather | bytes 4160 | tf_op jit(solution)/shard_map/all_gather | solution.py:68
  156.3 47.4 %all-gather = f32[64,4,4]{2,1,0:T(4,128)S(1)} all-gather(f32[1,4,4]{2,1,0:T(4,128)S(1)} %bitcast.46), channel_id=1, replica_groups=mesh['grp'=64,'tp'=8] {'grp'}, dimensions={0}, use_global_device_ids=true | all-gather | bytes 4160 | tf_op jit(solution)/shard_map/all_gather | solution.py:67
  203.9 0.1 select_reduce_fusion.4
  204.0 0.7 copy.71
  204.7 0.7 copy.80
  205.4 3.1 %fusion.13 = (bf16[8,1,1,512,128]{4,3,2,1,0:T(8,128)(2,1)}, bf16[8,1,1,512,128]{4,3,2,1,0:T(8,128)(2,1)}) fusion(bf16[8,2,1,512,128]{4,3,2,1,0:T(8,128)(2,1)} %param.10), kind=kLoop, calls=%fused_computation.39 | loop fusion | bytes 4194304 | tf_op jit(solution)/shard_map/slice | solution.py:15
  208.5 2.7 %reshape.234 = bf16[8,1024,64]{2,1,0:T(8,128)(2,1)S(1)} reshape(bf16[8,1,1,512,128]{4,3,2,1,0:T(8,128)(2,1)} %get-tuple-element.15) | data formatting | bytes 2097152 | tf_op jit(solution)/shard_map/reshape.2
  211.2 0.1 fusion.7
  211.4 0.7 select_reduce_fusion.1
  212.1 0.1 copy.67
  212.2 0.7 copy.68
  212.9 0.2 convert_reduce_fusion
  213.1 0.1 copy.77
  213.2 0.7 copy.78
  213.9 2.7 %reshape.236 = bf16[8,1024,64]{2,1,0:T(8,128)(2,1)S(1)} reshape(bf16[8,1,1,512,128]{4,3,2,1,0:T(8,128)(2,1)} %get-tuple-element.16) | data formatting | bytes 2097152 | tf_op jit(solution)/shard_map/reshape.18
  216.6 1.3 multiply_add_fusion
  217.9 0.7 copy-done.1
  218.6 0.6 broadcast.96
  219.2 2.2 reduce.8
  221.4 1.1 reshape.264
  222.5 1.9 copy.74
  224.5 1.2 copy.75
  225.7 0.4 select_reduce_fusion
  226.1 1.1 fusion.3
  227.2 0.1 convert_element_type.60
  227.3 0.9 fusion.15
  228.2 34.4 %reduce-scatter.2.cloned.1.call-done = f32[8,256]{1,0:T(8,128)} async-done(((f32[8,2048]{1,0:T(8,128)}), f32[8,256]{1,0:T(8,128)}) %reduce-scatter.2.cloned.1.call-update) | async-done | bytes 8208 | tf_op jit(solution)/shard_map/reduce_scatter | solution.py:87
  262.6 1.3 convert_element_type.61
  (31 shorter events, 0.5 us)
Async XLA Ops:
  6.5 220.8 %copy-start = (bf16[256,2048]{1,0:T(8,128)(2,1)S(1)}, bf16[256,2048]{1,0:T(8,128)(2,1)}, u32[]{:S(2)}) copy-start(bf16[256,2048]{1,0:T(8,128)(2,1)} %param.15) | copy-start | bytes 3145732
  95.8 10.5 %copy-start.6 = (s32[8]{0:T(128)S(1)}, s32[8]{0:T(128)}, u32[]{:S(2)}) copy-start(s32[8]{0:T(128)} %param.13) | copy-start | bytes 100
  95.8 10.6 %copy-start.4 = (bf16[8,256]{1,0:T(8,128)(2,1)S(1)}, bf16[8,256]{1,0:T(8,128)(2,1)}, u32[]{:S(2)}) copy-start(bf16[8,256]{1,0:T(8,128)(2,1)} %param.8) | copy-start | bytes 12292
  95.8 10.8 %copy-start.5 = (bf16[8,2,64]{2,1,0:T(2,128)(2,1)S(1)}, bf16[8,2,64]{2,1,0:T(2,128)(2,1)}, u32[]{:S(2)}) copy-start(bf16[8,2,64]{2,1,0:T(2,128)(2,1)} %param.9) | copy-start | bytes 6148
  97.9 120.1 %all-to-all-start = ((f32[64,1,1024]{2,1,0:T(1,128)}), f32[64,1,1024]{2,1,0:T(1,128)S(1)}, u32[]{:S(2)}, u32[]{:S(2)}) async-start(f32[64,1,1024]{2,1,0:T(1,128)} %reshape.263), calls=%async_computation | async-start | bytes 524288 | tf_op jit(solution)/shard_map/all_to_all | solution.py:70
  106.2 156.4 %reduce-scatter.2.cloned.1.call-start = ((), (), s32[]{:S(2)}) async-start(), calls=%async_computation.2 | async-start | bytes 73728 | tf_op jit(solution)/shard_map/reduce_scatter | solution.py:87
  203.9 4.6 %copy-start.2 = (pred[8,256]{1,0:T(8,128)(4,1)}, pred[8,256]{1,0:T(8,128)(4,1)S(1)}, u32[]{:S(2)}) copy-start(pred[8,256]{1,0:T(8,128)(4,1)S(1)} %broadcast_compare_fusion) | copy-start | bytes 6148
  216.6 9.1 %copy-start.3 = (pred[8,256]{1,0:T(8,128)(4,1)S(1)}, pred[8,256]{1,0:T(8,128)(4,1)}, u32[]{:S(2)}) copy-start(pred[8,256]{1,0:T(8,128)(4,1)} %copy-done.2) | copy-start | bytes 6148
  217.9 0.7 copy-start.1
Sparse Core Ops, SparseCore 0:
  228.3 34.2 reduce-scatter.1
